TPU v7x, 32 devices: a whole 2x2x4 slice. The times are simulated.
32 devices in a mesh: gx: 4 (over y, core), gy: 8 (over z, x).
Axes of the slice: x: 2, y: 2, z: 4, core: 2. Of those that a mesh axis runs over, the one named last changes fastest.
Arguments:
- velocity: float32 [3, 32, 64, 128], P(None, 'gx', 'gy'), may hold values from -6 to 6
- viscosity: float32 [32, 64, 128], P('gx', 'gy'), may hold values from 0.02 to 0.16
- forcing: float32 [4, 3, 32, 64, 128], P(None, None, 'gx', 'gy'), may hold values from -6 to 6
- earlier: float32 [60, 3, 32, 64, 128], P(None, None, 'gx', 'gy'), may hold values from -12 to 12
Outputs:
- velocity_out: float32 [3, 32, 64, 128], P(None, 'gx', 'gy')
- basis: float32 [64, 3, 32, 64, 128], P(None, None, 'gx', 'gy')
- factor: float32 [64, 64], replicated
All inputs are finite; a program needn't handle non-finite values.
Results may differ from a plain program's by a relative error of at most 0.000068.
Values sent between devices are 32-bit elements; how exact they have to be, the bound alone decides.
No kernel may reach another device: no remote copies, remote signals or barrier semaphores. Data moves between devices by JAX's collectives and lax.ppermute only.
A program may use at most 64 MiB of HBM per device.

v0:
```python
import jax
import jax.numpy as jnp
from jax import lax
from jax.sharding import PartitionSpec as P


def padded_2(array, sides, width):
    for axis, dim in sides:
        count, length = (lax.axis_size(axis), array.shape[dim])
        up = [(i, (i + 1) % count) for i in range(count - 1)]
        down = [(j, i) for i, j in up]
        last = lax.slice_in_dim(array, length - width, length, axis=dim)
        initial = lax.slice_in_dim(array, 0, width, axis=dim)
        before = lax.ppermute(last, axis, up)
        after = lax.ppermute(initial, axis, down)
        array = jnp.concatenate([before, array, after], axis=dim)
    return array


def laplace(padded, visc_pad):
    size_x = padded.shape[1] - 2
    size_y = padded.shape[2] - 2
    size_z = padded.shape[3] - 2
    centre = padded[:, 1 : 1 + size_x, 1 : 1 + size_y, 1 : 1 + size_z]
    visc_mid = visc_pad[1 : 1 + size_x, 1 : 1 + size_y, 1 : 1 + size_z]
    result = jnp.zeros_like(centre)
    for offset in ((2, 1, 1), (0, 1, 1), (1, 2, 1), (1, 0, 1), (1, 1, 2), (1, 1, 0)):
        first, second, third = offset
        beside = padded[:, first : first + size_x, second : second + size_y, third : third + size_z]
        visc_beside = visc_pad[
            first : first + size_x, second : second + size_y, third : third + size_z
        ]
        result = result + 0.5 * (visc_mid + visc_beside) * (beside - centre)
    return result


def factorize(panel, total_rows):
    local_gram = (
        lax.dot_general(
            panel,
            panel,
            (((1,), (1,)), ((), ())),
            precision=lax.Precision.HIGHEST,
            preferred_element_type=jnp.float32,
        )
        / total_rows
    )
    lower_factor = jnp.linalg.cholesky(lax.psum(local_gram, ("gx", "gy")))
    basis = jax.scipy.linalg.solve_triangular(lower_factor, panel, lower=True)
    return (lower_factor, basis)


def fields_rim_each(velocity, viscosity, forcing):
    visc_halo = padded_2(viscosity, (("gx", 0), ("gy", 1)), 1)
    visc_pad = jnp.pad(visc_halo, ((0, 0), (0, 0), (1, 1)))
    field = velocity
    fields = []
    for index in range(forcing.shape[0]):
        field_halo = padded_2(field, (("gx", 1), ("gy", 2)), 1)
        padded = jnp.pad(field_halo, ((0, 0), (0, 0), (0, 0), (1, 1)))
        field = field + laplace(padded, visc_pad) + forcing[index]
        fields.append(field)
    return fields


def local(velocity, viscosity, forcing, earlier):
    cell_rows = velocity.shape[0] * velocity.shape[1] * velocity.shape[2] * velocity.shape[3]
    total_rows = cell_rows * lax.axis_size("gx") * lax.axis_size("gy")
    fields = fields_rim_each(velocity, viscosity, forcing)
    panel_old = earlier.reshape(earlier.shape[0], cell_rows)
    snapshots = [field.reshape(1, cell_rows) for field in fields]
    lower_factor, basis = factorize(jnp.concatenate([panel_old] + snapshots, 0), total_rows)
    return (fields[-1], basis.reshape((basis.shape[0],) + velocity.shape), lower_factor.T)


def solution(mesh):
    return jax.shard_map(
        local,
        mesh=mesh,
        in_specs=(
            P(None, "gx", "gy", None),
            P("gx", "gy", None),
            P(None, None, "gx", "gy", None),
            P(None, None, "gx", "gy", None),
        ),
        out_specs=(P(None, "gx", "gy", None), P(None, None, "gx", "gy", None), P()),
        check_vma=False,
    )
```

profile of v0, /device:TPU:0, one launch (start us, length us, event | category | flops | bytes accessed | tf_op | source)
XLA Modules:
  0.0 195.6 jit_solution(2520877468651563737)
XLA Ops:
  1.5 2.6 %collective-permute-start.2 = (f32[1,8,128]{2,1,0:T(8,128)S(1)}, f32[1,8,128]{2,1,0:T(8,128)S(1)}, u32[]{:S(2)}, u32[]{:S(2)}) collective-permute-start(f32[1,8,128]{2,1,0:T(8,128)S(1)} %get-tuple-element.39), channel_id=1, source_target_pairs={{0,8},{8,16},{16,24},{1,9},{9,17},{17,25},{2,10},{10,18},{18,26},{... | collective-permute-start | bytes 12296 | tf_op jit(solution)/shard_map/ppermute | solution.py:14
  5.4 3.9 %collective-permute-done = f32[1,8,128]{2,1,0:T(8,128)S(1)} collective-permute-done((f32[1,8,128]{2,1,0:T(8,128)S(1)}, f32[1,8,128]{2,1,0:T(8,128)S(1)}, u32[]{:S(2)}, u32[]{:S(2)}) %collective-permute-start) | collective-permute-done | bytes 4128 | tf_op jit(solution)/shard_map/ppermute | solution.py:15
  10.2 3.4 %collective-permute-start.6 = (f32[10,1,128]{2,1,0:T(1,128)S(1)}, f32[10,1,128]{2,1,0:T(1,128)S(1)}, u32[]{:S(2)}, u32[]{:S(2)}) collective-permute-start(f32[10,1,128]{2,1,0:T(1,128)S(1)} %get-tuple-element.29), channel_id=1, source_target_pairs={{0,1},{1,2},{2,3},{3,4},{4,5},{5,6},{6,7},{8,9},{9,10},{10,11},{11... | collective-permute-start | bytes 15368 | tf_op jit(solution)/shard_map/ppermute | solution.py:14
  16.9 4.6 %collective-permute-start.3 = (f32[3,1,8,128]{3,2,1,0:T(8,128)S(1)}, f32[3,1,8,128]{3,2,1,0:T(8,128)S(1)}, u32[]{:S(2)}, u32[]{:S(2)}) collective-permute-start(f32[3,1,8,128]{3,2,1,0:T(8,128)S(1)} %get-tuple-element.26), channel_id=1, source_target_pairs={{0,8},{8,16},{16,24},{1,9},{9,17},{17,25},{2,10},{10,18},{18,26},{... | collective-permute-start | bytes 36872 | tf_op jit(solution)/shard_map/ppermute | solution.py:14
  23.3 4.3 %collective-permute-start.7 = (f32[3,10,1,128]{3,2,1,0:T(1,128)S(1)}, f32[3,10,1,128]{3,2,1,0:T(1,128)S(1)}, u32[]{:S(2)}, u32[]{:S(2)}) collective-permute-start(f32[3,10,1,128]{3,2,1,0:T(1,128)S(1)} %get-tuple-element.17), channel_id=1, source_target_pairs={{0,1},{1,2},{2,3},{3,4},{4,5},{5,6},{6,7},{8,9},{9,10},{10,11},{11... | collective-permute-start | bytes 46088 | tf_op jit(solution)/shard_map/ppermute | solution.py:14
  29.8 3.9 %collective-permute-done.5 = f32[3,10,1,128]{3,2,1,0:T(1,128)S(1)} collective-permute-done((f32[3,10,1,128]{3,2,1,0:T(1,128)S(1)}, f32[3,10,1,128]{3,2,1,0:T(1,128)S(1)}, u32[]{:S(2)}, u32[]{:S(2)}) %collective-permute-start.5) | collective-permute-done | bytes 15392 | tf_op jit(solution)/shard_map/ppermute | solution.py:15
  39.0 4.7 %collective-permute-done.8 = f32[3,1,8,128]{3,2,1,0:T(8,128)S(1)} collective-permute-done((f32[3,1,8,128]{3,2,1,0:T(8,128)S(1)}, f32[3,1,8,128]{3,2,1,0:T(8,128)S(1)}, u32[]{:S(2)}, u32[]{:S(2)}) %collective-permute-start.8) | collective-permute-done | bytes 12320 | tf_op jit(solution)/shard_map/ppermute | solution.py:15
  43.7 4.8 %collective-permute-start.11 = (f32[3,10,1,128]{3,2,1,0:T(1,128)S(1)}, f32[3,10,1,128]{3,2,1,0:T(1,128)S(1)}, u32[]{:S(2)}, u32[]{:S(2)}) collective-permute-start(f32[3,10,1,128]{3,2,1,0:T(1,128)S(1)} %get-tuple-element.15), channel_id=1, source_target_pairs={{0,1},{1,2},{2,3},{3,4},{4,5},{5,6},{6,7},{8,9},{9,10},{10,11},{11... | collective-permute-start | bytes 46088 | tf_op jit(solution)/shard_map/ppermute | solution.py:14
  50.0 4.2 %collective-permute-done.10 = f32[3,10,1,128]{3,2,1,0:T(1,128)S(1)} collective-permute-done((f32[3,10,1,128]{3,2,1,0:T(1,128)S(1)}, f32[3,10,1,128]{3,2,1,0:T(1,128)S(1)}, u32[]{:S(2)}, u32[]{:S(2)}) %collective-permute-start.10) | collective-permute-done | bytes 15392 | tf_op jit(solution)/shard_map/ppermute | solution.py:15
  55.6 2.9 %collective-permute-start.13 = (f32[3,1,8,128]{3,2,1,0:T(8,128)S(1)}, f32[3,1,8,128]{3,2,1,0:T(8,128)S(1)}, u32[]{:S(2)}, u32[]{:S(2)}) collective-permute-start(f32[3,1,8,128]{3,2,1,0:T(8,128)S(1)} %get-tuple-element.21), channel_id=1, source_target_pairs={{0,8},{8,16},{16,24},{1,9},{9,17},{17,25},{2,10},{10,18},{18,26},{... | collective-permute-start | bytes 36872 | tf_op jit(solution)/shard_map/ppermute | solution.py:14
  59.8 2.7 %collective-permute-done.12 = f32[3,1,8,128]{3,2,1,0:T(8,128)S(1)} collective-permute-done((f32[3,1,8,128]{3,2,1,0:T(8,128)S(1)}, f32[3,1,8,128]{3,2,1,0:T(8,128)S(1)}, u32[]{:S(2)}, u32[]{:S(2)}) %collective-permute-start.12) | collective-permute-done | bytes 12320 | tf_op jit(solution)/shard_map/ppermute | solution.py:15
  62.5 2.9 %collective-permute-start.15 = (f32[3,10,1,128]{3,2,1,0:T(1,128)S(1)}, f32[3,10,1,128]{3,2,1,0:T(1,128)S(1)}, u32[]{:S(2)}, u32[]{:S(2)}) collective-permute-start(f32[3,10,1,128]{3,2,1,0:T(1,128)S(1)} %get-tuple-element.13), channel_id=1, source_target_pairs={{0,1},{1,2},{2,3},{3,4},{4,5},{5,6},{6,7},{8,9},{9,10},{10,11},{11... | collective-permute-start | bytes 46088 | tf_op jit(solution)/shard_map/ppermute | solution.py:14
  66.9 4.2 %collective-permute-done.14 = f32[3,10,1,128]{3,2,1,0:T(1,128)S(1)} collective-permute-done((f32[3,10,1,128]{3,2,1,0:T(1,128)S(1)}, f32[3,10,1,128]{3,2,1,0:T(1,128)S(1)}, u32[]{:S(2)}, u32[]{:S(2)}) %collective-permute-start.14) | collective-permute-done | bytes 15392 | tf_op jit(solution)/shard_map/ppermute | solution.py:15
  72.5 3.2 %collective-permute-start.17 = (f32[3,1,8,128]{3,2,1,0:T(8,128)S(1)}, f32[3,1,8,128]{3,2,1,0:T(8,128)S(1)}, u32[]{:S(2)}, u32[]{:S(2)}) collective-permute-start(f32[3,1,8,128]{3,2,1,0:T(8,128)S(1)} %get-tuple-element.19), channel_id=1, source_target_pairs={{0,8},{8,16},{16,24},{1,9},{9,17},{17,25},{2,10},{10,18},{18,26},{... | collective-permute-start | bytes 36872 | tf_op jit(solution)/shard_map/ppermute | solution.py:14
  79.5 4.8 %collective-permute-start.19 = (f32[3,10,1,128]{3,2,1,0:T(1,128)S(1)}, f32[3,10,1,128]{3,2,1,0:T(1,128)S(1)}, u32[]{:S(2)}, u32[]{:S(2)}) collective-permute-start(f32[3,10,1,128]{3,2,1,0:T(1,128)S(1)} %get-tuple-element.11), channel_id=1, source_target_pairs={{0,1},{1,2},{2,3},{3,4},{4,5},{5,6},{6,7},{8,9},{9,10},{10,11},{11... | collective-permute-start | bytes 46088 | tf_op jit(solution)/shard_map/ppermute | solution.py:14
  86.6 6.3 %copy.21 = f32[8,8,192,128]{3,1,2,0:T(8,128)} copy(f32[8,8,192,128]{3,2,1,0:T(8,128)S(1)} %bitcast.40) | data formatting | bytes 12582912
  94.3 17.8 %concatenate.123 = f32[64,24576]{1,0:T(8,128)} concatenate(f32[60,24576]{1,0:T(8,128)} %bitcast.38, f32[1,24576]{1,0:T(1,128)S(1)} %bitcast.42, f32[1,24576]{1,0:T(1,128)S(1)} %bitcast.43, f32[1,24576]{1,0:T(1,128)S(1)} %bitcast.44, f32[1,24576]{1,0:T(1,128)S(1)} %bitcast.45), dimensions={0} | concatenate | bytes 12582912 | tf_op jit(solution)/shard_map/concatenate | solution.py:72
  112.1 8.2 %convolution_multiply_fusion = f32[64,64]{0,1:T(8,128)S(1)} fusion(f32[64,24576]{1,0:T(8,128)} %concatenate.123), kind=kOutput, calls=%fused_computation.2 | convolution fusion | flops 1207963648 | bytes 6307840 | tf_op jit(solution)/shard_map/dot_general | solution.py:39
  120.2 42.6 %psum.7 = f32[64,64]{0,1:T(8,128)S(1)} all-reduce(f32[64,64]{0,1:T(8,128)S(1)} %convolution_multiply_fusion), channel_id=1, replica_groups=mesh['gx'=4,'gy'=8] {'gx','gy'}, use_global_device_ids=true, to_apply=%region_0.1 | all-reduce | flops 4096 | bytes 32768 | tf_op jit(solution)/shard_map/psum | solution.py:48
  163.0 5.8 %cholesky.16 = f32[64,64]{1,0:T(8,128)S(1)} custom-call(f32[64,64]{1,0:T(8,128)S(1)} %fusion.83), custom_call_target="Cholesky" | custom-call | tf_op jit(solution)/shard_map/jit(cholesky)/cholesky | solution.py:48
  170.8 4.9 %custom-call.7 = f32[1,64,64]{1,2,0:T(8,128)S(1)} custom-call(f32[1,64,64]{2,1,0:T(8,128)S(1)} %get-tuple-element.32), custom_call_target="InvertDiagBlocksLowerTriangular" | custom-call | tf_op jit(solution)/shard_map/jit(_solve_triangular)/triangular_solve | solution.py:49
  175.7 3.9 %copy.22 = f32[8,8,192,128]{3,2,1,0:T(8,128)S(1)} copy(f32[8,8,192,128]{3,1,2,0:T(8,128)} %bitcast.37) | data formatting | bytes 12582912
  179.7 9.3 %fusion = f32[64,3,8,8,128]{4,0,3,2,1:T(8,128)S(1)} fusion(f32[3,8,8,128,64]{3,2,1,0,4:T(8,128)S(1)} %bitcast.39, f32[1,64,64]{1,2,0:T(8,128)S(1)} %custom-call.7), kind=kOutput, calls=%fused_computation | convolution fusion | flops 1207959552 | bytes 12599296 | tf_op jit(solution)/shard_map/jit(_solve_triangular)/triangular_solve | solution.py:49
  189.0 6.6 %copy.16 = f32[64,3,8,8,128]{4,3,2,1,0:T(8,128)} copy(f32[64,3,8,8,128]{4,0,3,2,1:T(8,128)S(1)} %fusion) | data formatting | bytes 12582912
  (62 shorter events, 31.9 us)
Async XLA Ops:
  0.6 85.0 %copy-start = (f32[60,3,8,8,128]{4,3,2,1,0:T(8,128)S(1)}, f32[60,3,8,8,128]{4,3,2,1,0:T(8,128)}, u32[]{:S(2)}) copy-start(f32[60,3,8,8,128]{4,3,2,1,0:T(8,128)} %param.7) | copy-start | bytes 17694724
  1.5 3.9 %collective-permute-start.2 = (f32[1,8,128]{2,1,0:T(8,128)S(1)}, f32[1,8,128]{2,1,0:T(8,128)S(1)}, u32[]{:S(2)}, u32[]{:S(2)}) collective-permute-start(f32[1,8,128]{2,1,0:T(8,128)S(1)} %get-tuple-element.39), channel_id=1, source_target_pairs={{0,8},{8,16},{16,24},{1,9},{9,17},{17,25},{2,10},{10,18},{18,26},{... | collective-permute-start | bytes 12296 | tf_op jit(solution)/shard_map/ppermute | solution.py:14
  4.1 5.2 %collective-permute-start = (f32[1,8,128]{2,1,0:T(8,128)S(1)}, f32[1,8,128]{2,1,0:T(8,128)S(1)}, u32[]{:S(2)}, u32[]{:S(2)}) collective-permute-start(f32[1,8,128]{2,1,0:T(8,128)S(1)} %get-tuple-element.38), channel_id=1, source_target_pairs={{8,0},{16,8},{24,16},{9,1},{17,9},{25,17},{10,2},{18,10},{26,18},{... | collective-permute-start | bytes 12296 | tf_op jit(solution)/shard_map/ppermute | solution.py:15
  10.2 11.3 %collective-permute-start.6 = (f32[10,1,128]{2,1,0:T(1,128)S(1)}, f32[10,1,128]{2,1,0:T(1,128)S(1)}, u32[]{:S(2)}, u32[]{:S(2)}) collective-permute-start(f32[10,1,128]{2,1,0:T(1,128)S(1)} %get-tuple-element.29), channel_id=1, source_target_pairs={{0,1},{1,2},{2,3},{3,4},{4,5},{5,6},{6,7},{8,9},{9,10},{10,11},{11... | collective-permute-start | bytes 15368 | tf_op jit(solution)/shard_map/ppermute | solution.py:14
  13.6 8.0 %collective-permute-start.4 = (f32[10,1,128]{2,1,0:T(1,128)S(1)}, f32[10,1,128]{2,1,0:T(1,128)S(1)}, u32[]{:S(2)}, u32[]{:S(2)}) collective-permute-start(f32[10,1,128]{2,1,0:T(1,128)S(1)} %get-tuple-element.30), channel_id=1, source_target_pairs={{1,0},{2,1},{3,2},{4,3},{5,4},{6,5},{7,6},{9,8},{10,9},{11,10},{12... | collective-permute-start | bytes 15368 | tf_op jit(solution)/shard_map/ppermute | solution.py:15
  15.6 7.6 %collective-permute-start.1 = (f32[3,1,8,128]{3,2,1,0:T(8,128)S(1)}, f32[3,1,8,128]{3,2,1,0:T(8,128)S(1)}, u32[]{:S(2)}, u32[]{:S(2)}) collective-permute-start(f32[3,1,8,128]{3,2,1,0:T(8,128)S(1)} %get-tuple-element.25), channel_id=1, source_target_pairs={{8,0},{16,8},{24,16},{9,1},{17,9},{25,17},{10,2},{18,10},{26,18},{... | collective-permute-start | bytes 36872 | tf_op jit(solution)/shard_map/ppermute | solution.py:15
  16.9 5.4 %collective-permute-start.3 = (f32[3,1,8,128]{3,2,1,0:T(8,128)S(1)}, f32[3,1,8,128]{3,2,1,0:T(8,128)S(1)}, u32[]{:S(2)}, u32[]{:S(2)}) collective-permute-start(f32[3,1,8,128]{3,2,1,0:T(8,128)S(1)} %get-tuple-element.26), channel_id=1, source_target_pairs={{0,8},{8,16},{16,24},{1,9},{9,17},{17,25},{2,10},{10,18},{18,26},{... | collective-permute-start | bytes 36872 | tf_op jit(solution)/shard_map/ppermute | solution.py:14
  23.3 6.4 %collective-permute-start.7 = (f32[3,10,1,128]{3,2,1,0:T(1,128)S(1)}, f32[3,10,1,128]{3,2,1,0:T(1,128)S(1)}, u32[]{:S(2)}, u32[]{:S(2)}) collective-permute-start(f32[3,10,1,128]{3,2,1,0:T(1,128)S(1)} %get-tuple-element.17), channel_id=1, source_target_pairs={{0,1},{1,2},{2,3},{3,4},{4,5},{5,6},{6,7},{8,9},{9,10},{10,11},{11... | collective-permute-start | bytes 46088 | tf_op jit(solution)/shard_map/ppermute | solution.py:14
  27.6 6.1 %collective-permute-start.5 = (f32[3,10,1,128]{3,2,1,0:T(1,128)S(1)}, f32[3,10,1,128]{3,2,1,0:T(1,128)S(1)}, u32[]{:S(2)}, u32[]{:S(2)}) collective-permute-start(f32[3,10,1,128]{3,2,1,0:T(1,128)S(1)} %get-tuple-element.18), channel_id=1, source_target_pairs={{1,0},{2,1},{3,2},{4,3},{5,4},{6,5},{7,6},{9,8},{10,9},{11,10},{12... | collective-permute-start | bytes 46088 | tf_op jit(solution)/shard_map/ppermute | solution.py:15
  35.2 3.8 %collective-permute-start.9 = (f32[3,1,8,128]{3,2,1,0:T(8,128)S(1)}, f32[3,1,8,128]{3,2,1,0:T(8,128)S(1)}, u32[]{:S(2)}, u32[]{:S(2)}) collective-permute-start(f32[3,1,8,128]{3,2,1,0:T(8,128)S(1)} %get-tuple-element.23), channel_id=1, source_target_pairs={{0,8},{8,16},{16,24},{1,9},{9,17},{17,25},{2,10},{10,18},{18,26},{... | collective-permute-start | bytes 36872 | tf_op jit(solution)/shard_map/ppermute | solution.py:14
  37.7 6.0 %collective-permute-start.8 = (f32[3,1,8,128]{3,2,1,0:T(8,128)S(1)}, f32[3,1,8,128]{3,2,1,0:T(8,128)S(1)}, u32[]{:S(2)}, u32[]{:S(2)}) collective-permute-start(f32[3,1,8,128]{3,2,1,0:T(8,128)S(1)} %get-tuple-element.24), channel_id=1, source_target_pairs={{8,0},{16,8},{24,16},{9,1},{17,9},{25,17},{10,2},{18,10},{26,18},{... | collective-permute-start | bytes 36872 | tf_op jit(solution)/shard_map/ppermute | solution.py:15
  43.7 6.2 %collective-permute-start.11 = (f32[3,10,1,128]{3,2,1,0:T(1,128)S(1)}, f32[3,10,1,128]{3,2,1,0:T(1,128)S(1)}, u32[]{:S(2)}, u32[]{:S(2)}) collective-permute-start(f32[3,10,1,128]{3,2,1,0:T(1,128)S(1)} %get-tuple-element.15), channel_id=1, source_target_pairs={{0,1},{1,2},{2,3},{3,4},{4,5},{5,6},{6,7},{8,9},{9,10},{10,11},{11... | collective-permute-start | bytes 46088 | tf_op jit(solution)/shard_map/ppermute | solution.py:14
  48.6 5.6 %collective-permute-start.10 = (f32[3,10,1,128]{3,2,1,0:T(1,128)S(1)}, f32[3,10,1,128]{3,2,1,0:T(1,128)S(1)}, u32[]{:S(2)}, u32[]{:S(2)}) collective-permute-start(f32[3,10,1,128]{3,2,1,0:T(1,128)S(1)} %get-tuple-element.16), channel_id=1, source_target_pairs={{1,0},{2,1},{3,2},{4,3},{5,4},{6,5},{7,6},{9,8},{10,9},{11,10},{12... | collective-permute-start | bytes 46088 | tf_op jit(solution)/shard_map/ppermute | solution.py:15
  55.6 4.2 %collective-permute-start.13 = (f32[3,1,8,128]{3,2,1,0:T(8,128)S(1)}, f32[3,1,8,128]{3,2,1,0:T(8,128)S(1)}, u32[]{:S(2)}, u32[]{:S(2)}) collective-permute-start(f32[3,1,8,128]{3,2,1,0:T(8,128)S(1)} %get-tuple-element.21), channel_id=1, source_target_pairs={{0,8},{8,16},{16,24},{1,9},{9,17},{17,25},{2,10},{10,18},{18,26},{... | collective-permute-start | bytes 36872 | tf_op jit(solution)/shard_map/ppermute | solution.py:14
  58.5 4.0 %collective-permute-start.12 = (f32[3,1,8,128]{3,2,1,0:T(8,128)S(1)}, f32[3,1,8,128]{3,2,1,0:T(8,128)S(1)}, u32[]{:S(2)}, u32[]{:S(2)}) collective-permute-start(f32[3,1,8,128]{3,2,1,0:T(8,128)S(1)} %get-tuple-element.22), channel_id=1, source_target_pairs={{8,0},{16,8},{24,16},{9,1},{17,9},{25,17},{10,2},{18,10},{26,18},{... | collective-permute-start | bytes 36872 | tf_op jit(solution)/shard_map/ppermute | solution.py:15
  62.5 4.4 %collective-permute-start.15 = (f32[3,10,1,128]{3,2,1,0:T(1,128)S(1)}, f32[3,10,1,128]{3,2,1,0:T(1,128)S(1)}, u32[]{:S(2)}, u32[]{:S(2)}) collective-permute-start(f32[3,10,1,128]{3,2,1,0:T(1,128)S(1)} %get-tuple-element.13), channel_id=1, source_target_pairs={{0,1},{1,2},{2,3},{3,4},{4,5},{5,6},{6,7},{8,9},{9,10},{10,11},{11... | collective-permute-start | bytes 46088 | tf_op jit(solution)/shard_map/ppermute | solution.py:14
  65.5 5.6 %collective-permute-start.14 = (f32[3,10,1,128]{3,2,1,0:T(1,128)S(1)}, f32[3,10,1,128]{3,2,1,0:T(1,128)S(1)}, u32[]{:S(2)}, u32[]{:S(2)}) collective-permute-start(f32[3,10,1,128]{3,2,1,0:T(1,128)S(1)} %get-tuple-element.14), channel_id=1, source_target_pairs={{1,0},{2,1},{3,2},{4,3},{5,4},{6,5},{7,6},{9,8},{10,9},{11,10},{12... | collective-permute-start | bytes 46088 | tf_op jit(solution)/shard_map/ppermute | solution.py:15
  72.5 4.5 %collective-permute-start.17 = (f32[3,1,8,128]{3,2,1,0:T(8,128)S(1)}, f32[3,1,8,128]{3,2,1,0:T(8,128)S(1)}, u32[]{:S(2)}, u32[]{:S(2)}) collective-permute-start(f32[3,1,8,128]{3,2,1,0:T(8,128)S(1)} %get-tuple-element.19), channel_id=1, source_target_pairs={{0,8},{8,16},{16,24},{1,9},{9,17},{17,25},{2,10},{10,18},{18,26},{... | collective-permute-start | bytes 36872 | tf_op jit(solution)/shard_map/ppermute | solution.py:14
  75.7 3.8 %collective-permute-start.16 = (f32[3,1,8,128]{3,2,1,0:T(8,128)S(1)}, f32[3,1,8,128]{3,2,1,0:T(8,128)S(1)}, u32[]{:S(2)}, u32[]{:S(2)}) collective-permute-start(f32[3,1,8,128]{3,2,1,0:T(8,128)S(1)} %get-tuple-element.20), channel_id=1, source_target_pairs={{8,0},{16,8},{24,16},{9,1},{17,9},{25,17},{10,2},{18,10},{26,18},{... | collective-permute-start | bytes 36872 | tf_op jit(solution)/shard_map/ppermute | solution.py:15
  79.5 13.4 %collective-permute-start.19 = (f32[3,10,1,128]{3,2,1,0:T(1,128)S(1)}, f32[3,10,1,128]{3,2,1,0:T(1,128)S(1)}, u32[]{:S(2)}, u32[]{:S(2)}) collective-permute-start(f32[3,10,1,128]{3,2,1,0:T(1,128)S(1)} %get-tuple-element.11), channel_id=1, source_target_pairs={{0,1},{1,2},{2,3},{3,4},{4,5},{5,6},{6,7},{8,9},{9,10},{10,11},{11... | collective-permute-start | bytes 46088 | tf_op jit(solution)/shard_map/ppermute | solution.py:14
  84.3 8.6 %collective-permute-start.18 = (f32[3,10,1,128]{3,2,1,0:T(1,128)S(1)}, f32[3,10,1,128]{3,2,1,0:T(1,128)S(1)}, u32[]{:S(2)}, u32[]{:S(2)}) collective-permute-start(f32[3,10,1,128]{3,2,1,0:T(1,128)S(1)} %get-tuple-element.12), channel_id=1, source_target_pairs={{1,0},{2,1},{3,2},{4,3},{5,4},{6,5},{7,6},{9,8},{10,9},{11,10},{12... | collective-permute-start | bytes 46088 | tf_op jit(solution)/shard_map/ppermute | solution.py:15
  94.3 17.8 %copy-start.1 = (f32[3,8,8,128]{3,2,1,0:T(8,128)}, f32[3,8,8,128]{3,2,1,0:T(8,128)S(1)}, u32[]{:S(2)}) copy-start(f32[3,8,8,128]{3,2,1,0:T(8,128)S(1)} %fusion.7) | copy-start | bytes 294916
where the time goes:
time: 197 us; the launch traced here: 196 us
  starting transfers between devices  49 us (25%)
  blocking collectives  42.6 us (22%)
  local copies, waits for them, and re-layouts  38.9 us (20%)
  waiting for transfers between devices  27 us (14%)
  other arithmetic  19.6 us (10%)
  matrix products  17.5 us (9%)
    psum x1, blocking collectives, factorize(): lower_factor = jnp.linalg.cholesky(lax.psum(local_gram, ('gx', 'gy')))  42.6 us
    ppermute x10, starting transfers between devices, padded_2(): before = lax.ppermute(last, axis, up)  36.1 us
    ppermute x10, waiting for transfers between devices, padded_2(): after = lax.ppermute(initial, axis, down)  26.1 us
    unnamed x12, local copies, waits for them, and re-layouts  19.4 us
    concatenate x1, local copies, waits for them, and re-layouts, local(): jnp.concatenate([panel_old] + snapshots, 0)  17.8 us
    ppermute x10, starting transfers between devices, padded_2(): after = lax.ppermute(initial, axis, down)  12.9 us
    another operation x1, matrix products, factorize(): basis = jax.scipy.linalg.solve_triangular(lower_factor, panel, lower=True)  9.33 us
    dot_general x1, matrix products, factorize(): lax.dot_general(panel, panel, (((1,), (1,)), ((), ())), precision=lax.Pre...  8.18 us
  transfers between devices with their start and end apart: 20, of which 10 were waited for; matrix products, arithmetic and copies ran while one was open for 5% of the time, Pallas kernels for 0%

commit v1 on v0

--- a/solution.py
+++ b/solution.py
@@ -45,7 +45,7 @@
         )
         / total_rows
     )
-    lower_factor = jnp.linalg.cholesky(lax.psum(local_gram, ("gx", "gy")))
+    lower_factor = jnp.linalg.cholesky(jnp.sum(lax.all_gather(local_gram, ("gx", "gy")), axis=0))
     basis = jax.scipy.linalg.solve_triangular(lower_factor, panel, lower=True)
     return (lower_factor, basis)
 

time: 197 us -> 227 us (1.15)
  blocking collectives: 42.6 us -> 72.8 us
    all_gather x0 -> x1, blocking collectives: none -> 72.8 us  [factorize(): lax.all_gather(local_gram, ('gx', 'gy'))]
    psum x1 -> x0, blocking collectives: 42.6 us -> none  [factorize(): lower_factor = jnp.linalg.cholesky(lax.psum(local_gram, ('gx', 'gy')))]
  transfers between devices with their start and end apart: 20 -> 20, of which waited for: 10 -> 10; matrix products, arithmetic and copies ran while one was open for 5% -> 4% of each run, Pallas kernels for 0% -> 0%
where the time goes in v1:
time: 227 us; the launch traced here: 226 us
  blocking collectives  72.8 us (32%)
  starting transfers between devices  49 us (22%)
  local copies, waits for them, and re-layouts  38.6 us (17%)
  waiting for transfers between devices  27 us (12%)
  other arithmetic  19.7 us (9%)
  matrix products  17.5 us (8%)
    all_gather x1, blocking collectives, factorize(): lax.all_gather(local_gram, ('gx', 'gy'))  72.8 us
    ppermute x10, starting transfers between devices, padded_2(): before = lax.ppermute(last, axis, up)  36.1 us
    ppermute x10, waiting for transfers between devices, padded_2(): after = lax.ppermute(initial, axis, down)  26.1 us
    unnamed x12, local copies, waits for them, and re-layouts  19.1 us
    concatenate x1, local copies, waits for them, and re-layouts, local(): jnp.concatenate([panel_old] + snapshots, 0)  17.8 us
    ppermute x10, starting transfers between devices, padded_2(): after = lax.ppermute(initial, axis, down)  12.9 us
    another operation x1, matrix products, factorize(): basis = jax.scipy.linalg.solve_triangular(lower_factor, panel, lower=True)  9.33 us
    dot_general x1, matrix products, factorize(): lax.dot_general(panel, panel, (((1,), (1,)), ((), ())), precision=lax.Pre...  8.16 us
  transfers between devices with their start and end apart: 20, of which 10 were waited for; matrix products, arithmetic and copies ran while one was open for 4% of the time, Pallas kernels for 0%

profile of v1, /device:TPU:0, one launch (start us, length us, event | category | flops | bytes accessed | tf_op | source)
XLA Modules:
  0.0 225.8 jit_solution(3379607018065146620)
XLA Ops:
  1.5 2.6 %collective-permute-start.2 = (f32[1,8,128]{2,1,0:T(8,128)S(1)}, f32[1,8,128]{2,1,0:T(8,128)S(1)}, u32[]{:S(2)}, u32[]{:S(2)}) collective-permute-start(f32[1,8,128]{2,1,0:T(8,128)S(1)} %get-tuple-element.42), channel_id=1, source_target_pairs={{0,8},{8,16},{16,24},{1,9},{9,17},{17,25},{2,10},{10,18},{18,26},{... | collective-permute-start | bytes 12296 | tf_op jit(solution)/shard_map/ppermute | solution.py:14
  5.4 3.9 %collective-permute-done = f32[1,8,128]{2,1,0:T(8,128)S(1)} collective-permute-done((f32[1,8,128]{2,1,0:T(8,128)S(1)}, f32[1,8,128]{2,1,0:T(8,128)S(1)}, u32[]{:S(2)}, u32[]{:S(2)}) %collective-permute-start) | collective-permute-done | bytes 4128 | tf_op jit(solution)/shard_map/ppermute | solution.py:15
  10.2 3.4 %collective-permute-start.6 = (f32[10,1,128]{2,1,0:T(1,128)S(1)}, f32[10,1,128]{2,1,0:T(1,128)S(1)}, u32[]{:S(2)}, u32[]{:S(2)}) collective-permute-start(f32[10,1,128]{2,1,0:T(1,128)S(1)} %get-tuple-element.32), channel_id=1, source_target_pairs={{0,1},{1,2},{2,3},{3,4},{4,5},{5,6},{6,7},{8,9},{9,10},{10,11},{11... | collective-permute-start | bytes 15368 | tf_op jit(solution)/shard_map/ppermute | solution.py:14
  16.9 4.6 %collective-permute-start.3 = (f32[3,1,8,128]{3,2,1,0:T(8,128)S(1)}, f32[3,1,8,128]{3,2,1,0:T(8,128)S(1)}, u32[]{:S(2)}, u32[]{:S(2)}) collective-permute-start(f32[3,1,8,128]{3,2,1,0:T(8,128)S(1)} %get-tuple-element.29), channel_id=1, source_target_pairs={{0,8},{8,16},{16,24},{1,9},{9,17},{17,25},{2,10},{10,18},{18,26},{... | collective-permute-start | bytes 36872 | tf_op jit(solution)/shard_map/ppermute | solution.py:14
  23.3 4.3 %collective-permute-start.7 = (f32[3,10,1,128]{3,2,1,0:T(1,128)S(1)}, f32[3,10,1,128]{3,2,1,0:T(1,128)S(1)}, u32[]{:S(2)}, u32[]{:S(2)}) collective-permute-start(f32[3,10,1,128]{3,2,1,0:T(1,128)S(1)} %get-tuple-element.20), channel_id=1, source_target_pairs={{0,1},{1,2},{2,3},{3,4},{4,5},{5,6},{6,7},{8,9},{9,10},{10,11},{11... | collective-permute-start | bytes 46088 | tf_op jit(solution)/shard_map/ppermute | solution.py:14
  29.8 3.9 %collective-permute-done.5 = f32[3,10,1,128]{3,2,1,0:T(1,128)S(1)} collective-permute-done((f32[3,10,1,128]{3,2,1,0:T(1,128)S(1)}, f32[3,10,1,128]{3,2,1,0:T(1,128)S(1)}, u32[]{:S(2)}, u32[]{:S(2)}) %collective-permute-start.5) | collective-permute-done | bytes 15392 | tf_op jit(solution)/shard_map/ppermute | solution.py:15
  39.0 4.7 %collective-permute-done.8 = f32[3,1,8,128]{3,2,1,0:T(8,128)S(1)} collective-permute-done((f32[3,1,8,128]{3,2,1,0:T(8,128)S(1)}, f32[3,1,8,128]{3,2,1,0:T(8,128)S(1)}, u32[]{:S(2)}, u32[]{:S(2)}) %collective-permute-start.8) | collective-permute-done | bytes 12320 | tf_op jit(solution)/shard_map/ppermute | solution.py:15
  43.7 4.8 %collective-permute-start.11 = (f32[3,10,1,128]{3,2,1,0:T(1,128)S(1)}, f32[3,10,1,128]{3,2,1,0:T(1,128)S(1)}, u32[]{:S(2)}, u32[]{:S(2)}) collective-permute-start(f32[3,10,1,128]{3,2,1,0:T(1,128)S(1)} %get-tuple-element.18), channel_id=1, source_target_pairs={{0,1},{1,2},{2,3},{3,4},{4,5},{5,6},{6,7},{8,9},{9,10},{10,11},{11... | collective-permute-start | bytes 46088 | tf_op jit(solution)/shard_map/ppermute | solution.py:14
  50.0 4.2 %collective-permute-done.10 = f32[3,10,1,128]{3,2,1,0:T(1,128)S(1)} collective-permute-done((f32[3,10,1,128]{3,2,1,0:T(1,128)S(1)}, f32[3,10,1,128]{3,2,1,0:T(1,128)S(1)}, u32[]{:S(2)}, u32[]{:S(2)}) %collective-permute-start.10) | collective-permute-done | bytes 15392 | tf_op jit(solution)/shard_map/ppermute | solution.py:15
  55.6 2.9 %collective-permute-start.13 = (f32[3,1,8,128]{3,2,1,0:T(8,128)S(1)}, f32[3,1,8,128]{3,2,1,0:T(8,128)S(1)}, u32[]{:S(2)}, u32[]{:S(2)}) collective-permute-start(f32[3,1,8,128]{3,2,1,0:T(8,128)S(1)} %get-tuple-element.24), channel_id=1, source_target_pairs={{0,8},{8,16},{16,24},{1,9},{9,17},{17,25},{2,10},{10,18},{18,26},{... | collective-permute-start | bytes 36872 | tf_op jit(solution)/shard_map/ppermute | solution.py:14
  59.8 2.7 %collective-permute-done.12 = f32[3,1,8,128]{3,2,1,0:T(8,128)S(1)} collective-permute-done((f32[3,1,8,128]{3,2,1,0:T(8,128)S(1)}, f32[3,1,8,128]{3,2,1,0:T(8,128)S(1)}, u32[]{:S(2)}, u32[]{:S(2)}) %collective-permute-start.12) | collective-permute-done | bytes 12320 | tf_op jit(solution)/shard_map/ppermute | solution.py:15
  62.5 2.9 %collective-permute-start.15 = (f32[3,10,1,128]{3,2,1,0:T(1,128)S(1)}, f32[3,10,1,128]{3,2,1,0:T(1,128)S(1)}, u32[]{:S(2)}, u32[]{:S(2)}) collective-permute-start(f32[3,10,1,128]{3,2,1,0:T(1,128)S(1)} %get-tuple-element.16), channel_id=1, source_target_pairs={{0,1},{1,2},{2,3},{3,4},{4,5},{5,6},{6,7},{8,9},{9,10},{10,11},{11... | collective-permute-start | bytes 46088 | tf_op jit(solution)/shard_map/ppermute | solution.py:14
  66.9 4.2 %collective-permute-done.14 = f32[3,10,1,128]{3,2,1,0:T(1,128)S(1)} collective-permute-done((f32[3,10,1,128]{3,2,1,0:T(1,128)S(1)}, f32[3,10,1,128]{3,2,1,0:T(1,128)S(1)}, u32[]{:S(2)}, u32[]{:S(2)}) %collective-permute-start.14) | collective-permute-done | bytes 15392 | tf_op jit(solution)/shard_map/ppermute | solution.py:15
  72.5 3.2 %collective-permute-start.17 = (f32[3,1,8,128]{3,2,1,0:T(8,128)S(1)}, f32[3,1,8,128]{3,2,1,0:T(8,128)S(1)}, u32[]{:S(2)}, u32[]{:S(2)}) collective-permute-start(f32[3,1,8,128]{3,2,1,0:T(8,128)S(1)} %get-tuple-element.22), channel_id=1, source_target_pairs={{0,8},{8,16},{16,24},{1,9},{9,17},{17,25},{2,10},{10,18},{18,26},{... | collective-permute-start | bytes 36872 | tf_op jit(solution)/shard_map/ppermute | solution.py:14
  79.5 4.8 %collective-permute-start.19 = (f32[3,10,1,128]{3,2,1,0:T(1,128)S(1)}, f32[3,10,1,128]{3,2,1,0:T(1,128)S(1)}, u32[]{:S(2)}, u32[]{:S(2)}) collective-permute-start(f32[3,10,1,128]{3,2,1,0:T(1,128)S(1)} %get-tuple-element.14), channel_id=1, source_target_pairs={{0,1},{1,2},{2,3},{3,4},{4,5},{5,6},{6,7},{8,9},{9,10},{10,11},{11... | collective-permute-start | bytes 46088 | tf_op jit(solution)/shard_map/ppermute | solution.py:14
  86.6 6.3 %copy.23 = f32[8,8,192,128]{3,1,2,0:T(8,128)} copy(f32[8,8,192,128]{3,2,1,0:T(8,128)S(1)} %bitcast.41) | data formatting | bytes 12582912
  94.3 17.8 %concatenate.123 = f32[64,24576]{1,0:T(8,128)} concatenate(f32[60,24576]{1,0:T(8,128)} %bitcast.39, f32[1,24576]{1,0:T(1,128)S(1)} %bitcast.44, f32[1,24576]{1,0:T(1,128)S(1)} %bitcast.45, f32[1,24576]{1,0:T(1,128)S(1)} %bitcast.46, f32[1,24576]{1,0:T(1,128)S(1)} %bitcast.47), dimensions={0} | concatenate | bytes 12582912 | tf_op jit(solution)/shard_map/concatenate | solution.py:72
  112.1 8.2 %convolution_multiply_fusion = f32[64,64]{1,0:T(8,128)S(1)} fusion(f32[64,24576]{1,0:T(8,128)} %concatenate.123), kind=kOutput, calls=%fused_computation.2 | convolution fusion | flops 1207963648 | bytes 6307840 | tf_op jit(solution)/shard_map/dot_general | solution.py:39
  120.2 72.8 %all-gather = f32[2048,64]{1,0:T(8,128)S(1)} all-gather(f32[64,64]{1,0:T(8,128)S(1)} %convolution_multiply_fusion), channel_id=2, replica_groups=mesh['gx'=4,'gy'=8] {'gx','gy'}, dimensions={0}, use_global_device_ids=true | all-gather | bytes 540672 | tf_op jit(solution)/shard_map/all_gather | solution.py:48
  193.2 5.8 %cholesky.16 = f32[64,64]{1,0:T(8,128)S(1)} custom-call(f32[64,64]{1,0:T(8,128)S(1)} %fusion.83), custom_call_target="Cholesky" | custom-call | tf_op jit(solution)/shard_map/jit(cholesky)/cholesky | solution.py:48
  201.1 4.9 %custom-call.7 = f32[1,64,64]{1,2,0:T(8,128)S(1)} custom-call(f32[1,64,64]{2,1,0:T(8,128)S(1)} %get-tuple-element.35), custom_call_target="InvertDiagBlocksLowerTriangular" | custom-call | tf_op jit(solution)/shard_map/jit(_solve_triangular)/triangular_solve | solution.py:49
  206.0 3.9 %copy.24 = f32[8,8,192,128]{3,2,1,0:T(8,128)S(1)} copy(f32[8,8,192,128]{3,1,2,0:T(8,128)} %bitcast.38) | data formatting | bytes 12582912
  209.9 9.3 %fusion = f32[64,3,8,8,128]{4,0,3,2,1:T(8,128)S(1)} fusion(f32[3,8,8,128,64]{3,2,1,0,4:T(8,128)S(1)} %bitcast.40, f32[1,64,64]{1,2,0:T(8,128)S(1)} %custom-call.7), kind=kOutput, calls=%fused_computation | convolution fusion | flops 1207959552 | bytes 12599296 | tf_op jit(solution)/shard_map/jit(_solve_triangular)/triangular_solve | solution.py:49
  219.5 6.3 %copy.19 = f32[64,3,8,8,128]{4,3,2,1,0:T(8,128)} copy(f32[64,3,8,8,128]{4,0,3,2,1:T(8,128)S(1)} %fusion) | data formatting | bytes 12582912
  (63 shorter events, 32.0 us)
Async XLA Ops:
  0.6 85.0 %copy-start = (f32[60,3,8,8,128]{4,3,2,1,0:T(8,128)S(1)}, f32[60,3,8,8,128]{4,3,2,1,0:T(8,128)}, u32[]{:S(2)}) copy-start(f32[60,3,8,8,128]{4,3,2,1,0:T(8,128)} %param.7) | copy-start | bytes 17694724
  1.5 3.9 %collective-permute-start.2 = (f32[1,8,128]{2,1,0:T(8,128)S(1)}, f32[1,8,128]{2,1,0:T(8,128)S(1)}, u32[]{:S(2)}, u32[]{:S(2)}) collective-permute-start(f32[1,8,128]{2,1,0:T(8,128)S(1)} %get-tuple-element.42), channel_id=1, source_target_pairs={{0,8},{8,16},{16,24},{1,9},{9,17},{17,25},{2,10},{10,18},{18,26},{... | collective-permute-start | bytes 12296 | tf_op jit(solution)/shard_map/ppermute | solution.py:14
  4.1 5.2 %collective-permute-start = (f32[1,8,128]{2,1,0:T(8,128)S(1)}, f32[1,8,128]{2,1,0:T(8,128)S(1)}, u32[]{:S(2)}, u32[]{:S(2)}) collective-permute-start(f32[1,8,128]{2,1,0:T(8,128)S(1)} %get-tuple-element.41), channel_id=1, source_target_pairs={{8,0},{16,8},{24,16},{9,1},{17,9},{25,17},{10,2},{18,10},{26,18},{... | collective-permute-start | bytes 12296 | tf_op jit(solution)/shard_map/ppermute | solution.py:15
  10.2 11.3 %collective-permute-start.6 = (f32[10,1,128]{2,1,0:T(1,128)S(1)}, f32[10,1,128]{2,1,0:T(1,128)S(1)}, u32[]{:S(2)}, u32[]{:S(2)}) collective-permute-start(f32[10,1,128]{2,1,0:T(1,128)S(1)} %get-tuple-element.32), channel_id=1, source_target_pairs={{0,1},{1,2},{2,3},{3,4},{4,5},{5,6},{6,7},{8,9},{9,10},{10,11},{11... | collective-permute-start | bytes 15368 | tf_op jit(solution)/shard_map/ppermute | solution.py:14
  13.6 8.0 %collective-permute-start.4 = (f32[10,1,128]{2,1,0:T(1,128)S(1)}, f32[10,1,128]{2,1,0:T(1,128)S(1)}, u32[]{:S(2)}, u32[]{:S(2)}) collective-permute-start(f32[10,1,128]{2,1,0:T(1,128)S(1)} %get-tuple-element.33), channel_id=1, source_target_pairs={{1,0},{2,1},{3,2},{4,3},{5,4},{6,5},{7,6},{9,8},{10,9},{11,10},{12... | collective-permute-start | bytes 15368 | tf_op jit(solution)/shard_map/ppermute | solution.py:15
  15.6 7.6 %collective-permute-start.1 = (f32[3,1,8,128]{3,2,1,0:T(8,128)S(1)}, f32[3,1,8,128]{3,2,1,0:T(8,128)S(1)}, u32[]{:S(2)}, u32[]{:S(2)}) collective-permute-start(f32[3,1,8,128]{3,2,1,0:T(8,128)S(1)} %get-tuple-element.28), channel_id=1, source_target_pairs={{8,0},{16,8},{24,16},{9,1},{17,9},{25,17},{10,2},{18,10},{26,18},{... | collective-permute-start | bytes 36872 | tf_op jit(solution)/shard_map/ppermute | solution.py:15
  16.9 5.4 %collective-permute-start.3 = (f32[3,1,8,128]{3,2,1,0:T(8,128)S(1)}, f32[3,1,8,128]{3,2,1,0:T(8,128)S(1)}, u32[]{:S(2)}, u32[]{:S(2)}) collective-permute-start(f32[3,1,8,128]{3,2,1,0:T(8,128)S(1)} %get-tuple-element.29), channel_id=1, source_target_pairs={{0,8},{8,16},{16,24},{1,9},{9,17},{17,25},{2,10},{10,18},{18,26},{... | collective-permute-start | bytes 36872 | tf_op jit(solution)/shard_map/ppermute | solution.py:14
  23.3 6.4 %collective-permute-start.7 = (f32[3,10,1,128]{3,2,1,0:T(1,128)S(1)}, f32[3,10,1,128]{3,2,1,0:T(1,128)S(1)}, u32[]{:S(2)}, u32[]{:S(2)}) collective-permute-start(f32[3,10,1,128]{3,2,1,0:T(1,128)S(1)} %get-tuple-element.20), channel_id=1, source_target_pairs={{0,1},{1,2},{2,3},{3,4},{4,5},{5,6},{6,7},{8,9},{9,10},{10,11},{11... | collective-permute-start | bytes 46088 | tf_op jit(solution)/shard_map/ppermute | solution.py:14
  27.6 6.1 %collective-permute-start.5 = (f32[3,10,1,128]{3,2,1,0:T(1,128)S(1)}, f32[3,10,1,128]{3,2,1,0:T(1,128)S(1)}, u32[]{:S(2)}, u32[]{:S(2)}) collective-permute-start(f32[3,10,1,128]{3,2,1,0:T(1,128)S(1)} %get-tuple-element.21), channel_id=1, source_target_pairs={{1,0},{2,1},{3,2},{4,3},{5,4},{6,5},{7,6},{9,8},{10,9},{11,10},{12... | collective-permute-start | bytes 46088 | tf_op jit(solution)/shard_map/ppermute | solution.py:15
  35.2 3.8 %collective-permute-start.9 = (f32[3,1,8,128]{3,2,1,0:T(8,128)S(1)}, f32[3,1,8,128]{3,2,1,0:T(8,128)S(1)}, u32[]{:S(2)}, u32[]{:S(2)}) collective-permute-start(f32[3,1,8,128]{3,2,1,0:T(8,128)S(1)} %get-tuple-element.26), channel_id=1, source_target_pairs={{0,8},{8,16},{16,24},{1,9},{9,17},{17,25},{2,10},{10,18},{18,26},{... | collective-permute-start | bytes 36872 | tf_op jit(solution)/shard_map/ppermute | solution.py:14
  37.7 6.0 %collective-permute-start.8 = (f32[3,1,8,128]{3,2,1,0:T(8,128)S(1)}, f32[3,1,8,128]{3,2,1,0:T(8,128)S(1)}, u32[]{:S(2)}, u32[]{:S(2)}) collective-permute-start(f32[3,1,8,128]{3,2,1,0:T(8,128)S(1)} %get-tuple-element.27), channel_id=1, source_target_pairs={{8,0},{16,8},{24,16},{9,1},{17,9},{25,17},{10,2},{18,10},{26,18},{... | collective-permute-start | bytes 36872 | tf_op jit(solution)/shard_map/ppermute | solution.py:15
  43.7 6.2 %collective-permute-start.11 = (f32[3,10,1,128]{3,2,1,0:T(1,128)S(1)}, f32[3,10,1,128]{3,2,1,0:T(1,128)S(1)}, u32[]{:S(2)}, u32[]{:S(2)}) collective-permute-start(f32[3,10,1,128]{3,2,1,0:T(1,128)S(1)} %get-tuple-element.18), channel_id=1, source_target_pairs={{0,1},{1,2},{2,3},{3,4},{4,5},{5,6},{6,7},{8,9},{9,10},{10,11},{11... | collective-permute-start | bytes 46088 | tf_op jit(solution)/shard_map/ppermute | solution.py:14
  48.6 5.6 %collective-permute-start.10 = (f32[3,10,1,128]{3,2,1,0:T(1,128)S(1)}, f32[3,10,1,128]{3,2,1,0:T(1,128)S(1)}, u32[]{:S(2)}, u32[]{:S(2)}) collective-permute-start(f32[3,10,1,128]{3,2,1,0:T(1,128)S(1)} %get-tuple-element.19), channel_id=1, source_target_pairs={{1,0},{2,1},{3,2},{4,3},{5,4},{6,5},{7,6},{9,8},{10,9},{11,10},{12... | collective-permute-start | bytes 46088 | tf_op jit(solution)/shard_map/ppermute | solution.py:15
  55.6 4.2 %collective-permute-start.13 = (f32[3,1,8,128]{3,2,1,0:T(8,128)S(1)}, f32[3,1,8,128]{3,2,1,0:T(8,128)S(1)}, u32[]{:S(2)}, u32[]{:S(2)}) collective-permute-start(f32[3,1,8,128]{3,2,1,0:T(8,128)S(1)} %get-tuple-element.24), channel_id=1, source_target_pairs={{0,8},{8,16},{16,24},{1,9},{9,17},{17,25},{2,10},{10,18},{18,26},{... | collective-permute-start | bytes 36872 | tf_op jit(solution)/shard_map/ppermute | solution.py:14
  58.5 4.0 %collective-permute-start.12 = (f32[3,1,8,128]{3,2,1,0:T(8,128)S(1)}, f32[3,1,8,128]{3,2,1,0:T(8,128)S(1)}, u32[]{:S(2)}, u32[]{:S(2)}) collective-permute-start(f32[3,1,8,128]{3,2,1,0:T(8,128)S(1)} %get-tuple-element.25), channel_id=1, source_target_pairs={{8,0},{16,8},{24,16},{9,1},{17,9},{25,17},{10,2},{18,10},{26,18},{... | collective-permute-start | bytes 36872 | tf_op jit(solution)/shard_map/ppermute | solution.py:15
  62.5 4.4 %collective-permute-start.15 = (f32[3,10,1,128]{3,2,1,0:T(1,128)S(1)}, f32[3,10,1,128]{3,2,1,0:T(1,128)S(1)}, u32[]{:S(2)}, u32[]{:S(2)}) collective-permute-start(f32[3,10,1,128]{3,2,1,0:T(1,128)S(1)} %get-tuple-element.16), channel_id=1, source_target_pairs={{0,1},{1,2},{2,3},{3,4},{4,5},{5,6},{6,7},{8,9},{9,10},{10,11},{11... | collective-permute-start | bytes 46088 | tf_op jit(solution)/shard_map/ppermute | solution.py:14
  65.5 5.6 %collective-permute-start.14 = (f32[3,10,1,128]{3,2,1,0:T(1,128)S(1)}, f32[3,10,1,128]{3,2,1,0:T(1,128)S(1)}, u32[]{:S(2)}, u32[]{:S(2)}) collective-permute-start(f32[3,10,1,128]{3,2,1,0:T(1,128)S(1)} %get-tuple-element.17), channel_id=1, source_target_pairs={{1,0},{2,1},{3,2},{4,3},{5,4},{6,5},{7,6},{9,8},{10,9},{11,10},{12... | collective-permute-start | bytes 46088 | tf_op jit(solution)/shard_map/ppermute | solution.py:15
  72.5 4.5 %collective-permute-start.17 = (f32[3,1,8,128]{3,2,1,0:T(8,128)S(1)}, f32[3,1,8,128]{3,2,1,0:T(8,128)S(1)}, u32[]{:S(2)}, u32[]{:S(2)}) collective-permute-start(f32[3,1,8,128]{3,2,1,0:T(8,128)S(1)} %get-tuple-element.22), channel_id=1, source_target_pairs={{0,8},{8,16},{16,24},{1,9},{9,17},{17,25},{2,10},{10,18},{18,26},{... | collective-permute-start | bytes 36872 | tf_op jit(solution)/shard_map/ppermute | solution.py:14
  75.7 3.8 %collective-permute-start.16 = (f32[3,1,8,128]{3,2,1,0:T(8,128)S(1)}, f32[3,1,8,128]{3,2,1,0:T(8,128)S(1)}, u32[]{:S(2)}, u32[]{:S(2)}) collective-permute-start(f32[3,1,8,128]{3,2,1,0:T(8,128)S(1)} %get-tuple-element.23), channel_id=1, source_target_pairs={{8,0},{16,8},{24,16},{9,1},{17,9},{25,17},{10,2},{18,10},{26,18},{... | collective-permute-start | bytes 36872 | tf_op jit(solution)/shard_map/ppermute | solution.py:15
  79.5 13.4 %collective-permute-start.19 = (f32[3,10,1,128]{3,2,1,0:T(1,128)S(1)}, f32[3,10,1,128]{3,2,1,0:T(1,128)S(1)}, u32[]{:S(2)}, u32[]{:S(2)}) collective-permute-start(f32[3,10,1,128]{3,2,1,0:T(1,128)S(1)} %get-tuple-element.14), channel_id=1, source_target_pairs={{0,1},{1,2},{2,3},{3,4},{4,5},{5,6},{6,7},{8,9},{9,10},{10,11},{11... | collective-permute-start | bytes 46088 | tf_op jit(solution)/shard_map/ppermute | solution.py:14
  84.3 8.6 %collective-permute-start.18 = (f32[3,10,1,128]{3,2,1,0:T(1,128)S(1)}, f32[3,10,1,128]{3,2,1,0:T(1,128)S(1)}, u32[]{:S(2)}, u32[]{:S(2)}) collective-permute-start(f32[3,10,1,128]{3,2,1,0:T(1,128)S(1)} %get-tuple-element.15), channel_id=1, source_target_pairs={{1,0},{2,1},{3,2},{4,3},{5,4},{6,5},{7,6},{9,8},{10,9},{11,10},{12... | collective-permute-start | bytes 46088 | tf_op jit(solution)/shard_map/ppermute | solution.py:15
  94.3 17.8 %copy-start.1 = (f32[3,8,8,128]{3,2,1,0:T(8,128)}, f32[3,8,8,128]{3,2,1,0:T(8,128)S(1)}, u32[]{:S(2)}) copy-start(f32[3,8,8,128]{3,2,1,0:T(8,128)S(1)} %fusion.7) | copy-start | bytes 294916
